TPU v7x, 32 devices: a whole 2x2x4 slice. The times are simulated.
32 devices in a mesh: leaf: 8 (over y, x, core), panel: 4 (over z).
Axes of the slice: x: 2, y: 2, z: 4, core: 2. Of those that a mesh axis runs over, the one named last changes fastest.
Arguments:
- live_tiles: int32 [15], replicated, may hold values from 8 to 16
- row_tiles: int32 [14, 8], replicated, may hold values from 0 to 47, as said below
- rhs0: float32 [256, 16384], P('panel', 'leaf'), may hold values from -6 to 6
- rhs1: float32 [256, 8192], P('panel', 'leaf'), may hold values from -6 to 6
- rhs2: float32 [256, 4096], P('panel', 'leaf'), may hold values from -6 to 6
- rhs3: float32 [256, 2048], P('panel', 'leaf'), may hold values from -6 to 6
- dinv0: float32 [16384, 2048], P('leaf', 'panel'), as said below
- dinv1: float32 [8192, 2048], P('leaf', 'panel'), as said below
- dinv2: float32 [4096, 2048], P('leaf', 'panel'), as said below
- dinv3: float32 [2048, 2048], P('leaf', 'panel'), as said below
- off0: float32 [8192, 2048], P('leaf', 'panel'), may hold values from -0.125 to 0.125
- off1: float32 [4096, 2048], P('leaf', 'panel'), may hold values from -0.125 to 0.125
- off2: float32 [2048, 2048], P('leaf', 'panel'), may hold values from -0.125 to 0.125
Outputs:
- sol0: float32 [256, 16384], P('panel', 'leaf')
- sol1: float32 [256, 8192], P('panel', 'leaf')
- sol2: float32 [256, 4096], P('panel', 'leaf')
- sol3: float32 [256, 2048], P('panel', 'leaf')
Inputs may be any that keep to these rules, and one draw needn't show every extreme that they name: `row_tiles`: each row names 8 different tiles; for a supernode of level k every value is below (3 - k) * 16. `live_tiles`: counted level by level in the supernodes' order. `dinv0`: each 2048 x 2048 row block is lower triangular with diagonal entries from 0.5 to 2. `dinv1`: each 2048 x 2048 row block is lower triangular with diagonal entries from 0.5 to 2. `dinv2`: each 2048 x 2048 row block is lower triangular with diagonal entries from 0.5 to 2. `dinv3`: each 2048 x 2048 row block is lower triangular with diagonal entries from 0.5 to 2.
All inputs are finite; a program needn't handle non-finite values.
Results may differ from a plain program's by a relative error of at most 0.00028.
Values sent between devices are 32-bit elements; how exact they have to be, the bound alone decides.
A program may use at most 64 MiB of HBM per device.

v0:
```python
import jax
import jax.numpy as jnp
from jax import lax
from jax.sharding import PartitionSpec as P

B = 128
LEVELS = 4
highest = lax.Precision.HIGHEST


def swapped(block, axis, bit):
    count = lax.axis_size(axis)
    route = []
    for low in range(count):
        high = low | 1 << bit
        if high != low and high < count:
            route += [(low, high), (high, low)]
    return lax.ppermute(block, axis, route)


def leaf_bit(leaf_index, bit_number):
    return leaf_index // 2**bit_number % 2


def group_rows(vector, height, leaf_index):
    for bit_number in range(height):
        partner = swapped(vector, "leaf", bit_number)
        is_lower = leaf_bit(leaf_index, bit_number) == 0
        vector = jnp.where(
            is_lower, jnp.concatenate([vector, partner], 1), jnp.concatenate([partner, vector], 1)
        )
    return vector


def group_halving(buffer, height, leaf_index):
    for bit_number in reversed(range(height)):
        half_width = buffer.shape[1] // 2
        is_lower = leaf_bit(leaf_index, bit_number) == 0
        kept_half = jnp.where(is_lower, buffer[:, :half_width], buffer[:, half_width:])
        given_half = jnp.where(is_lower, buffer[:, half_width:], buffer[:, :half_width])
        buffer = kept_half + swapped(given_half, "leaf", bit_number)
    return buffer


def group_total(partial_sum, height):
    for bit_number in range(height):
        partial_sum = partial_sum + swapped(partial_sum, "leaf", bit_number)
    return partial_sum


def to_columns(vector, height, leaf_index):
    full_rows = group_rows(vector, height, leaf_index)
    return lax.all_to_all(full_rows, "panel", split_axis=1, concat_axis=0, tiled=True)


def contract_last(left, right):
    return lax.dot_general(
        left, right, (((1,), (1,)), ((), ())), precision=highest, preferred_element_type=jnp.float32
    )


def selector(chosen, offset, tile_count):
    return (chosen[:, None] == offset + jnp.arange(tile_count, dtype=jnp.int32)[None, :]).astype(
        jnp.float32
    )


def geometry(height, leaf_index, live_tiles, first_node, order_rows):
    group_width = 2**height
    node_index = leaf_index // group_width
    group_place = leaf_index % group_width
    rows_here = order_rows // group_width
    live_count = lax.dynamic_index_in_dim(live_tiles, first_node + node_index, keepdims=False)
    node_mask = (jnp.arange(order_rows, dtype=jnp.int32) < live_count * B).astype(jnp.float32)
    local_mask = lax.dynamic_slice_in_dim(node_mask, group_place * rows_here, rows_here)
    return (node_index, group_place, rows_here, node_mask, local_mask)


def chosen_tiles(row_tiles, first_node, node_index, group_place, local_tiles):
    entry = lax.dynamic_index_in_dim(row_tiles, first_node + node_index, keepdims=False)
    return lax.dynamic_slice_in_dim(entry, group_place * local_tiles, local_tiles)


def local(
    live_tiles, row_tiles, rhs0, rhs1, rhs2, rhs3, dinv0, dinv1, dinv2, dinv3, off0, off1, off2
):
    right_sides = [rhs0, rhs1, rhs2, rhs3]
    inverses = [dinv0, dinv1, dinv2, dinv3]
    off_rows = [off0, off1, off2]
    leaf_index = lax.axis_index("leaf")
    panel_index = lax.axis_index("panel")
    leaf_count = lax.axis_size("leaf")
    panel_count = lax.axis_size("panel")
    order_rows = dinv0.shape[0]
    tile_count = order_rows // B
    share_rows = rhs0.shape[0]
    all_rhs = share_rows * panel_count
    off_tiles = row_tiles.shape[1]
    first_nodes = []
    start_node = 0
    for height in range(LEVELS):
        first_nodes.append(start_node)
        start_node = start_node + leaf_count // 2**height
    buffers = [jnp.zeros((share_rows, order_rows), jnp.float32) for height in range(LEVELS)]
    columns_kept = []
    for height in range(LEVELS):
        node_index, group_place, rows_here, node_mask, local_mask = geometry(
            height, leaf_index, live_tiles, first_nodes[height], order_rows
        )
        residual = right_sides[height]
        if height > 0:
            residual = residual - group_halving(buffers[height], height, leaf_index)
        spread = to_columns(residual * local_mask[None, :], height, leaf_index)
        inverse = inverses[height]
        solved = lax.psum_scatter(
            contract_last(spread, inverse), "panel", scatter_dimension=0, tiled=True
        )
        columns = to_columns(solved * local_mask[None, :], height, leaf_index)
        columns_kept.append(columns)
        if height < LEVELS - 1:
            block_rows = off_rows[height]
            update = lax.psum_scatter(
                contract_last(columns, block_rows), "panel", scatter_dimension=0, tiled=True
            )
            local_tiles = off_tiles // 2**height
            chosen = chosen_tiles(
                row_tiles, first_nodes[height], node_index, group_place, local_tiles
            )
            pieces = update.reshape(share_rows, local_tiles, B)
            for ancestor in range(height + 1, LEVELS):
                picked = selector(chosen, (ancestor - height - 1) * tile_count, tile_count)
                sent = jnp.einsum("rtb,tc->rcb", pieces, picked, precision=highest)
                buffers[ancestor] = buffers[ancestor] + sent.reshape(share_rows, order_rows)
    full_solutions = [None] * LEVELS
    outputs = [None] * LEVELS
    for height in reversed(range(LEVELS)):
        node_index, group_place, rows_here, node_mask, local_mask = geometry(
            height, leaf_index, live_tiles, first_nodes[height], order_rows
        )
        target = columns_kept[height]
        if height < LEVELS - 1:
            local_tiles = off_tiles // 2**height
            chosen = chosen_tiles(
                row_tiles, first_nodes[height], node_index, group_place, local_tiles
            )
            gathered = jnp.zeros((all_rhs, local_tiles, B), jnp.float32)
            for ancestor in range(height + 1, LEVELS):
                picked = selector(chosen, (ancestor - height - 1) * tile_count, tile_count)
                above = full_solutions[ancestor].reshape(all_rhs, tile_count, B)
                gathered = gathered + jnp.einsum("rcb,tc->rtb", above, picked, precision=highest)
            correction = jnp.dot(
                gathered.reshape(all_rhs, local_tiles * B),
                off_rows[height],
                precision=highest,
                preferred_element_type=jnp.float32,
            )
            target = target - group_total(correction, height)
        whole_target = lax.all_gather(target, "panel", axis=1, tiled=True) * node_mask[None, :]
        mine = lax.dynamic_slice_in_dim(whole_target, group_place * rows_here, rows_here, 1)
        partial_sum = jnp.dot(
            mine, inverses[height], precision=highest, preferred_element_type=jnp.float32
        )
        partial_sum = group_total(partial_sum, height)
        whole_solution = (
            lax.all_gather(partial_sum, "panel", axis=1, tiled=True) * node_mask[None, :]
        )
        full_solutions[height] = whole_solution
        outputs[height] = lax.dynamic_slice(
            whole_solution,
            (panel_index * share_rows, group_place * rows_here),
            (share_rows, rows_here),
        )
    return tuple(outputs)


def solution(mesh):
    return jax.shard_map(
        local,
        mesh=mesh,
        in_specs=(
            P(),
            P(),
            P("panel", "leaf"),
            P("panel", "leaf"),
            P("panel", "leaf"),
            P("panel", "leaf"),
            P("leaf", "panel"),
            P("leaf", "panel"),
            P("leaf", "panel"),
            P("leaf", "panel"),
            P("leaf", "panel"),
            P("leaf", "panel"),
            P("leaf", "panel"),
        ),
        out_specs=(P("panel", "leaf"), P("panel", "leaf"), P("panel", "leaf"), P("panel", "leaf")),
        check_vma=False,
    )
```

profile of v0, /device:TPU:0, one launch (start us, length us, event | category | flops | bytes accessed | tf_op | source)
XLA Modules:
  0.0 909.9 jit_solution(4213799960495342376)
XLA Ops:
  10.6 20.6 %all_to_all.134 = f32[64,4,512]{2,0,1:T(8,128)S(1)} all-to-all(f32[64,4,512]{2,0,1:T(8,128)S(1)} %bitcast.207), channel_id=1, replica_groups=mesh['leaf'=8,'panel'=4] {'panel'}, dimensions={1} | all-to-all | bytes 1048576 | tf_op jit(solution)/shard_map/all_to_all | solution.py:53
  31.2 7.1 fusion.71
  38.4 42.8 %reduce-scatter.8.cloned.1.call-done = f32[64,2048]{1,0:T(8,128)} async-done(((f32[256,2048]{1,0:T(8,128)}), f32[64,2048]{1,0:T(8,128)}) %reduce-scatter.8.cloned.1.call-update) | async-done | bytes 524304 | tf_op jit(solution)/shard_map/reduce_scatter | solution.py:115
  82.5 17.5 %all_to_all.135 = f32[64,4,512]{2,0,1:T(8,128)S(1)} all-to-all(f32[64,4,512]{2,0,1:T(8,128)S(1)} %bitcast.209), channel_id=1, replica_groups=mesh['leaf'=8,'panel'=4] {'panel'}, dimensions={1} | all-to-all | bytes 1048576 | tf_op jit(solution)/shard_map/all_to_all | solution.py:53
  100.0 2.9 fusion.72
  103.2 25.9 %reduce-scatter.10.cloned.1.call-done = f32[64,1024]{1,0:T(8,128)} async-done(((f32[256,1024]{1,0:T(8,128)}), f32[64,1024]{1,0:T(8,128)}) %reduce-scatter.10.cloned.1.call-update) | async-done | bytes 262160 | tf_op jit(solution)/shard_map/reduce_scatter | solution.py:122
  136.2 17.5 %all_to_all.136 = f32[64,4,512]{2,0,1:T(8,128)S(1)} all-to-all(f32[64,4,512]{2,0,1:T(8,128)S(1)} %maximum_select_fusion), channel_id=1, replica_groups=mesh['leaf'=8,'panel'=4] {'panel'}, dimensions={1} | all-to-all | bytes 1048576 | tf_op jit(solution)/shard_map/all_to_all | solution.py:53
  153.7 2.9 fusion.73
  156.7 26.4 %reduce-scatter.12.cloned.1.call-done = f32[64,1024]{1,0:T(8,128)} async-done(((f32[256,1024]{1,0:T(8,128)}), f32[64,1024]{1,0:T(8,128)}) %reduce-scatter.12.cloned.1.call-update) | async-done | bytes 262160 | tf_op jit(solution)/shard_map/reduce_scatter | solution.py:115
  185.8 17.5 %all_to_all.137 = f32[64,4,512]{2,0,1:T(8,128)S(1)} all-to-all(f32[64,4,512]{2,0,1:T(8,128)S(1)} %maximum_select_fusion.1), channel_id=1, replica_groups=mesh['leaf'=8,'panel'=4] {'panel'}, dimensions={1} | all-to-all | bytes 1048576 | tf_op jit(solution)/shard_map/all_to_all | solution.py:53
  207.8 19.2 %reduce-scatter.14.cloned.1.call-done = f32[64,512]{1,0:T(8,128)} async-done(((f32[256,512]{1,0:T(8,128)}), f32[64,512]{1,0:T(8,128)}) %reduce-scatter.14.cloned.1.call-update) | async-done | bytes 131088 | tf_op jit(solution)/shard_map/reduce_scatter | solution.py:122
  230.8 5.0 collective-permute-done.3
  241.3 6.9 collective-permute-done.6
  248.3 16.7 %all_to_all.138 = f32[64,4,512]{2,0,1:T(8,128)S(1)} all-to-all(f32[64,4,512]{2,0,1:T(8,128)S(1)} %maximum_select_fusion.2), channel_id=1, replica_groups=mesh['leaf'=8,'panel'=4] {'panel'}, dimensions={1} | all-to-all | bytes 1048576 | tf_op jit(solution)/shard_map/all_to_all | solution.py:53
  267.0 20.9 %reduce-scatter.16.cloned.1.call-done = f32[64,512]{1,0:T(8,128)} async-done(((f32[256,512]{1,0:T(8,128)}), f32[64,512]{1,0:T(8,128)}) %reduce-scatter.16.cloned.1.call-update) | async-done | bytes 131088 | tf_op jit(solution)/shard_map/reduce_scatter | solution.py:115
  292.7 6.0 collective-permute-done.8
  298.8 16.6 %all_to_all.139 = f32[64,4,512]{2,0,1:T(8,128)S(1)} all-to-all(f32[64,4,512]{2,0,1:T(8,128)S(1)} %maximum_select_fusion.3), channel_id=1, replica_groups=mesh['leaf'=8,'panel'=4] {'panel'}, dimensions={1} | all-to-all | bytes 1048576 | tf_op jit(solution)/shard_map/all_to_all | solution.py:53
  315.4 2.4 fusion.76
  319.8 1.9 fusion.28
  321.7 15.2 %reduce-scatter.18.cloned.1.call-done = f32[64,256]{1,0:T(8,128)} async-done(((f32[256,256]{1,0:T(8,128)}), f32[64,256]{1,0:T(8,128)}) %reduce-scatter.18.cloned.1.call-update) | async-done | bytes 65552 | tf_op jit(solution)/shard_map/reduce_scatter | solution.py:122
  342.3 4.9 collective-permute-done.9
  350.0 3.1 collective-permute-done.10
  358.2 4.1 collective-permute-done.13
  363.9 6.0 collective-permute-done.14
  370.0 15.8 %all_to_all.140 = f32[64,4,512]{2,0,1:T(8,128)S(1)} all-to-all(f32[64,4,512]{2,0,1:T(8,128)S(1)} %maximum_select_fusion.4), channel_id=1, replica_groups=mesh['leaf'=8,'panel'=4] {'panel'}, dimensions={1} | all-to-all | bytes 1048576 | tf_op jit(solution)/shard_map/all_to_all | solution.py:53
  387.1 19.2 %reduce-scatter.20.cloned.1.call-done = f32[64,256]{1,0:T(8,128)} async-done(((f32[256,256]{1,0:T(8,128)}), f32[64,256]{1,0:T(8,128)}) %reduce-scatter.20.cloned.1.call-update) | async-done | bytes 65552 | tf_op jit(solution)/shard_map/reduce_scatter | solution.py:115
  409.9 4.1 collective-permute-done.16
  416.5 5.1 collective-permute-done.17
  421.7 16.5 %all_to_all.141 = f32[64,4,512]{2,0,1:T(8,128)} all-to-all(f32[64,4,512]{2,0,1:T(8,128)S(1)} %maximum_select_fusion.5), channel_id=1, replica_groups=mesh['leaf'=8,'panel'=4] {'panel'}, dimensions={1} | all-to-all | bytes 1048576 | tf_op jit(solution)/shard_map/all_to_all | solution.py:53
  438.3 44.8 %all-gather.9.cloned.1.call-done = f32[256,2048]{1,0:T(8,128)} async-done(((f32[256,512]{1,0:T(8,128)}), f32[256,2048]{1,0:T(8,128)}) %all-gather.9.cloned.1.call-update) | async-done | bytes 2097168 | tf_op jit(solution)/shard_map/all_gather | solution.py:158
  484.9 1.9 collective-permute-done.18
  488.4 12.5 %collective-permute-done.19 = f32[256,512]{1,0:T(8,128)S(1)} collective-permute-done((f32[256,512]{1,0:T(8,128)S(1)}, f32[256,512]{1,0:T(8,128)S(1)}, u32[]{:S(2)}, u32[]{:S(2)}) %collective-permute-start.19) | collective-permute-done | bytes 524320 | tf_op jit(solution)/shard_map/ppermute | solution.py:18
  502.5 11.6 %collective-permute-done.20 = f32[256,512]{1,0:T(8,128)S(1)} collective-permute-done((f32[256,512]{1,0:T(8,128)S(1)}, f32[256,512]{1,0:T(8,128)S(1)}, u32[]{:S(2)}, u32[]{:S(2)}) %collective-permute-start.20) | collective-permute-done | bytes 524320 | tf_op jit(solution)/shard_map/ppermute | solution.py:18
  515.1 44.6 %all-gather.11.cloned.1.call-done = f32[256,2048]{1,0:T(8,128)} async-done(((f32[256,512]{1,0:T(8,128)}), f32[256,2048]{1,0:T(8,128)}) %all-gather.11.cloned.1.call-update) | async-done | bytes 2097168 | tf_op jit(solution)/shard_map/all_gather | solution.py:165
  564.0 1.9 collective-permute-done.21
  567.6 12.5 %collective-permute-done.22 = f32[256,512]{1,0:T(8,128)S(1)} collective-permute-done((f32[256,512]{1,0:T(8,128)S(1)}, f32[256,512]{1,0:T(8,128)S(1)}, u32[]{:S(2)}, u32[]{:S(2)}) %collective-permute-start.22) | collective-permute-done | bytes 524320 | tf_op jit(solution)/shard_map/ppermute | solution.py:18
  581.3 44.4 %all-gather.13.cloned.1.call-done = f32[256,2048]{1,0:T(8,128)} async-done(((f32[256,512]{1,0:T(8,128)}), f32[256,2048]{1,0:T(8,128)}) %all-gather.13.cloned.1.call-update) | async-done | bytes 2097168 | tf_op jit(solution)/shard_map/all_gather | solution.py:158
  625.6 2.5 fusion.11
  631.7 12.5 %collective-permute-done.24 = f32[256,512]{1,0:T(8,128)S(1)} collective-permute-done((f32[256,512]{1,0:T(8,128)S(1)}, f32[256,512]{1,0:T(8,128)S(1)}, u32[]{:S(2)}, u32[]{:S(2)}) %collective-permute-start.24) | collective-permute-done | bytes 524320 | tf_op jit(solution)/shard_map/ppermute | solution.py:18
  645.2 44.6 %all-gather.15.cloned.1.call-done = f32[256,2048]{1,0:T(8,128)} async-done(((f32[256,512]{1,0:T(8,128)}), f32[256,2048]{1,0:T(8,128)}) %all-gather.15.cloned.1.call-update) | async-done | bytes 2097168 | tf_op jit(solution)/shard_map/all_gather | solution.py:165
  699.6 44.6 %all-gather.17.cloned.1.call-done = f32[256,2048]{1,0:T(8,128)} async-done(((f32[256,512]{1,0:T(8,128)}), f32[256,2048]{1,0:T(8,128)}) %all-gather.17.cloned.1.call-update) | async-done | bytes 2097168 | tf_op jit(solution)/shard_map/all_gather | solution.py:158
  744.2 3.2 fusion.5
  750.5 44.4 %all-gather.19.cloned.1.call-done = f32[256,2048]{1,0:T(8,128)} async-done(((f32[256,512]{1,0:T(8,128)}), f32[256,2048]{1,0:T(8,128)}) %all-gather.19.cloned.1.call-update) | async-done | bytes 2097168 | tf_op jit(solution)/shard_map/all_gather | solution.py:165
  801.9 2.8 convolution_subtract_fusion
  804.7 44.6 %all-gather.21.cloned.1.call-done = f32[256,2048]{1,0:T(8,128)} async-done(((f32[256,512]{1,0:T(8,128)}), f32[256,2048]{1,0:T(8,128)}) %all-gather.21.cloned.1.call-update) | async-done | bytes 2097168 | tf_op jit(solution)/shard_map/all_gather | solution.py:158
  849.3 7.3 fusion
  856.7 2.0 broadcast_multiply_fusion.2
  861.9 39.3 %all-gather.23.cloned.1.call-done = f32[256,2048]{1,0:T(8,128)} async-done(((f32[256,512]{1,0:T(8,128)}), f32[256,2048]{1,0:T(8,128)}) %all-gather.23.cloned.1.call-update) | async-done | bytes 2097168 | tf_op jit(solution)/shard_map/all_gather | solution.py:165
  (239 shorter events, 99.6 us)
Async XLA Ops:
  7.2 146.5 %copy-start = (f32[1024,512]{1,0:T(8,128)S(1)}, f32[1024,512]{1,0:T(8,128)}, u32[]{:S(2)}) copy-start(f32[1024,512]{1,0:T(8,128)} %param.20) | copy-start | bytes 6291460
  7.2 74.1 %reduce-scatter.8.cloned.1.call-start = ((), (), s32[]{:S(2)}) async-start(), calls=%async_computation.15 | async-start | bytes 2621440 | tf_op jit(solution)/shard_map/reduce_scatter | solution.py:115
  38.4 90.8 %reduce-scatter.10.cloned.1.call-start = ((), (), s32[]{:S(2)}) async-start(), calls=%async_computation.16 | async-start | bytes 1310720 | tf_op jit(solution)/shard_map/reduce_scatter | solution.py:122
  103.0 80.1 %reduce-scatter.12.cloned.1.call-start = ((), (), s32[]{:S(2)}) async-start(), calls=%async_computation.17 | async-start | bytes 1310720 | tf_op jit(solution)/shard_map/reduce_scatter | solution.py:115
  103.2 104.0 %copy-start.24 = (s32[8]{0:T(128)}, s32[8]{0:T(128)S(1)}, u32[]{:S(2)}) copy-start(s32[8]{0:T(128)S(1)} %dynamic-slice_reduce_fusion) | copy-start | bytes 100
  131.5 1.9 collective-permute-start
  132.2 50.9 %copy-start.19 = (f32[1024]{0:T(1024)}, f32[1024]{0:T(1024)S(1)}, u32[]{:S(2)}) copy-start(f32[1024]{0:T(1024)S(1)} %dynamic_slice.72) | copy-start | bytes 12292
  134.5 1.6 collective-permute-start.1
  156.6 70.4 %reduce-scatter.14.cloned.1.call-start = ((), (), s32[]{:S(2)}) async-start(), calls=%async_computation.18 | async-start | bytes 655360 | tf_op jit(solution)/shard_map/reduce_scatter | solution.py:122
  184.2 1.6 collective-permute-start.2
  206.0 81.9 %reduce-scatter.16.cloned.1.call-start = ((), (), s32[]{:S(2)}) async-start(), calls=%async_computation.19 | async-start | bytes 655360 | tf_op jit(solution)/shard_map/reduce_scatter | solution.py:115
  229.4 6.5 collective-permute-start.3
  235.9 1.4 collective-permute-start.4
  238.3 1.4 collective-permute-start.5
  239.7 8.5 collective-permute-start.6
  266.9 70.0 %reduce-scatter.18.cloned.1.call-start = ((), (), s32[]{:S(2)}) async-start(), calls=%async_computation.20 | async-start | bytes 327680 | tf_op jit(solution)/shard_map/reduce_scatter | solution.py:122
  288.8 1.4 collective-permute-start.7
  290.3 8.4 collective-permute-start.8
  317.8 88.5 %reduce-scatter.20.cloned.1.call-start = ((), (), s32[]{:S(2)}) async-start(), calls=%async_computation.21 | async-start | bytes 327680 | tf_op jit(solution)/shard_map/reduce_scatter | solution.py:115
  340.7 6.4 collective-permute-start.9
  347.9 5.2 collective-permute-start.10
  353.1 1.3 collective-permute-start.11
  355.3 1.3 collective-permute-start.12
  356.7 5.6 collective-permute-start.13
  362.3 7.6 collective-permute-start.14
  387.1 96.0 %all-gather.9.cloned.1.call-start = ((), (), s32[]{:S(2)}) async-start(), calls=%async_computation.22 | async-start | bytes 2621440 | tf_op jit(solution)/shard_map/all_gather | solution.py:158
  407.2 1.3 collective-permute-start.15
  408.4 5.6 collective-permute-start.16
  414.1 7.6 collective-permute-start.17
  438.2 121.5 %all-gather.11.cloned.1.call-start = ((), (), s32[]{:S(2)}) async-start(), calls=%async_computation.23 | async-start | bytes 2621440 | tf_op jit(solution)/shard_map/all_gather | solution.py:165
  484.8 2.0 collective-permute-start.18
  486.9 14.0 %collective-permute-start.19 = (f32[256,512]{1,0:T(8,128)S(1)}, f32[256,512]{1,0:T(8,128)S(1)}, u32[]{:S(2)}, u32[]{:S(2)}) collective-permute-start(f32[256,512]{1,0:T(8,128)S(1)} %add.290), channel_id=1, source_target_pairs={{0,8},{8,0},{4,12},{12,4},{16,24},{24,16},{20,28},{28,20},{1,9},{9... | collective-permute-start | bytes 1572872 | tf_op jit(solution)/shard_map/ppermute | solution.py:18
  501.0 13.2 %collective-permute-start.20 = (f32[256,512]{1,0:T(8,128)S(1)}, f32[256,512]{1,0:T(8,128)S(1)}, u32[]{:S(2)}, u32[]{:S(2)}) collective-permute-start(f32[256,512]{1,0:T(8,128)S(1)} %add.291), channel_id=1, source_target_pairs={{0,16},{16,0},{4,20},{20,4},{8,24},{24,8},{12,28},{28,12},{1,17},{... | collective-permute-start | bytes 1572872 | tf_op jit(solution)/shard_map/ppermute | solution.py:18
  515.1 110.6 %all-gather.13.cloned.1.call-start = ((), (), s32[]{:S(2)}) async-start(), calls=%async_computation.24 | async-start | bytes 2621440 | tf_op jit(solution)/shard_map/all_gather | solution.py:158
  564.0 61.7 %copy-start.23 = (f32[512]{0:T(512)S(1)}, f32[512]{0:T(512)}, u32[]{:S(2)}) copy-start(f32[512]{0:T(512)} %copy-done.21) | copy-start | bytes 6148
  564.0 2.0 collective-permute-start.21
  566.0 14.0 %collective-permute-start.22 = (f32[256,512]{1,0:T(8,128)S(1)}, f32[256,512]{1,0:T(8,128)S(1)}, u32[]{:S(2)}, u32[]{:S(2)}) collective-permute-start(f32[256,512]{1,0:T(8,128)S(1)} %add.293), channel_id=1, source_target_pairs={{0,8},{8,0},{4,12},{12,4},{16,24},{24,16},{20,28},{28,20},{1,9},{9... | collective-permute-start | bytes 1572872 | tf_op jit(solution)/shard_map/ppermute | solution.py:18
  581.0 108.7 %all-gather.15.cloned.1.call-start = ((), (), s32[]{:S(2)}) async-start(), calls=%async_computation.25 | async-start | bytes 2621440 | tf_op jit(solution)/shard_map/all_gather | solution.py:165
  628.1 61.6 %copy-start.18 = (f32[2048]{0:T(1024)S(1)}, f32[2048]{0:T(1024)}, u32[]{:S(2)}) copy-start(f32[2048]{0:T(1024)} %copy-done.17) | copy-start | bytes 24580
  628.1 2.0 collective-permute-start.23
  630.2 14.0 %collective-permute-start.24 = (f32[256,512]{1,0:T(8,128)S(1)}, f32[256,512]{1,0:T(8,128)S(1)}, u32[]{:S(2)}, u32[]{:S(2)}) collective-permute-start(f32[256,512]{1,0:T(8,128)S(1)} %add.295), channel_id=1, source_target_pairs={{0,8},{8,0},{4,12},{12,4},{16,24},{24,16},{20,28},{28,20},{1,9},{9... | collective-permute-start | bytes 1572872 | tf_op jit(solution)/shard_map/ppermute | solution.py:18
  645.1 99.1 %all-gather.17.cloned.1.call-start = ((), (), s32[]{:S(2)}) async-start(), calls=%async_computation.26 | async-start | bytes 2621440 | tf_op jit(solution)/shard_map/all_gather | solution.py:158
  695.5 48.6 %copy-start.20 = (f32[1024]{0:T(1024)S(1)}, f32[1024]{0:T(1024)}, u32[]{:S(2)}) copy-start(f32[1024]{0:T(1024)} %copy-done.19) | copy-start | bytes 12292
  696.6 2.0 collective-permute-start.25
  699.6 95.3 %all-gather.19.cloned.1.call-start = ((), (), s32[]{:S(2)}) async-start(), calls=%async_computation.27 | async-start | bytes 2621440 | tf_op jit(solution)/shard_map/all_gather | solution.py:165
  747.4 2.0 collective-permute-start.26
  750.2 99.1 %all-gather.21.cloned.1.call-start = ((), (), s32[]{:S(2)}) async-start(), calls=%async_computation.28 | async-start | bytes 2621440 | tf_op jit(solution)/shard_map/all_gather | solution.py:158
  804.7 96.6 %all-gather.23.cloned.1.call-start = ((), (), s32[]{:S(2)}) async-start(), calls=%async_computation.29 | async-start | bytes 2621440 | tf_op jit(solution)/shard_map/all_gather | solution.py:165
  (27 other events, 178.1 us)
Sparse Core Ops, SparseCore 0:
  38.5 42.7 reduce-scatter.7
  103.1 25.9 reduce-scatter.9
  156.7 26.3 reduce-scatter.11
  206.1 20.8 reduce-scatter.13
  267.0 20.8 reduce-scatter.15
  317.9 18.9 reduce-scatter.17
  387.2 19.0 reduce-scatter.19
  438.3 44.6 all-gather.8
  515.2 44.4 all-gather.10
  581.1 44.4 all-gather.12
  645.2 44.4 all-gather.14
  699.7 44.4 all-gather.16
  750.4 44.4 all-gather.18
  804.8 44.4 all-gather.20
  856.8 44.4 all-gather.22
where the time goes:
time: 919 us; the launch traced here: 910 us
  waiting for transfers between devices  635 us (69%)
  blocking collectives  139 us (15%)
  matrix products  51.3 us (6%)
  other arithmetic  26.6 us (3%)
  starting transfers between devices  22.7 us (2%)
  between operations  17.7 us (2%)
  local copies, waits for them, and re-layouts  17.6 us (2%)
    all_gather x4, waiting for transfers between devices, local(): lax.all_gather(target, 'panel', axis=1, tiled=True) * node_mask[None, :]  178 us
    all_gather x4, waiting for transfers between devices, local(): lax.all_gather(partial_sum, 'panel', axis=1, tiled=True)  173 us
    all_to_all x8, blocking collectives, to_columns(): lax.all_to_all(full_rows, 'panel', split_axis=1, concat_axis=0, tiled=True)  139 us
    ppermute x27, waiting for transfers between devices, swapped(): return lax.ppermute(block, axis, route)  114 us
    reduce_scatter x4, waiting for transfers between devices, local(): lax.psum_scatter(contract_last(spread, inverse), 'panel', scatter_dimensi...  109 us
    reduce_scatter x3, waiting for transfers between devices, local(): lax.psum_scatter(contract_last(columns, block_rows), 'panel', scatter_dim...  60.3 us
    ppermute x27, starting transfers between devices, swapped(): return lax.ppermute(block, axis, route)  21.2 us
    dot_general x7, matrix products, contract_last(): lax.dot_general(left, right, (((1,), (1,)), ((), ())), precision=highest,...  20.4 us
  transfers between devices with their start and end apart: 42, of which 42 were waited for; matrix products, arithmetic and copies ran while one was open for 1% of the time, Pallas kernels for 0%

commit v1 on v0

--- a/solution.py
+++ b/solution.py
@@ -6,6 +6,28 @@
 B = 128
 LEVELS = 4
 highest = lax.Precision.HIGHEST
+
+
+def joined_along(blocks, dim):
+    shape = list(blocks.shape[1:])
+    shape[dim] *= blocks.shape[0]
+    return jnp.moveaxis(blocks, 0, dim).reshape(shape)
+
+
+def ring_gather(array, axis, dim):
+    size = lax.axis_size(axis)
+    pairs = [(i, (i + 1) % size) for i in range(size)]
+    back = [(b, a) for a, b in pairs]
+    lower, upper = ([], [])
+    for step in range(size - 1):
+        if step % 2 == 0:
+            lower.append(lax.ppermute(lower[-1] if lower else array, axis, pairs))
+        else:
+            upper.append(lax.ppermute(upper[-1] if upper else array, axis, back))
+    blocks = jnp.stack([*lower[::-1], array, *upper])
+    shift = lax.axis_index(axis) - len(lower)
+    blocks = blocks[(jnp.arange(size) - shift) % size]
+    return joined_along(blocks, dim)
 
 
 def swapped(block, axis, bit):
@@ -161,9 +183,7 @@
             mine, inverses[height], precision=highest, preferred_element_type=jnp.float32
         )
         partial_sum = group_total(partial_sum, height)
-        whole_solution = (
-            lax.all_gather(partial_sum, "panel", axis=1, tiled=True) * node_mask[None, :]
-        )
+        whole_solution = ring_gather(partial_sum, "panel", 1) * node_mask[None, :]
         full_solutions[height] = whole_solution
         outputs[height] = lax.dynamic_slice(
             whole_solution,

time: 919 us -> 941 us (1.024)
  waiting for transfers between devices: 635 us -> 586 us
  local copies, waits for them, and re-layouts: 17.6 us -> 53.2 us
  starting transfers between devices: 22.7 us -> 42.9 us
  other arithmetic: 26.6 us -> 38.3 us
    all_gather x4 -> x0, waiting for transfers between devices: 173 us -> none  [local(): lax.all_gather(partial_sum, 'panel', axis=1, tiled=True)]
    ppermute x0 -> x12, waiting for transfers between devices: none -> 124 us  [the longest x8 103 us: ring_gather(): lower.append(lax.ppermute(lower[-1] if lower else array, axis, pairs))]
    ppermute x0 -> x12, starting transfers between devices: none -> 20.9 us  [the longest x4 14.6 us: ring_gather(): upper.append(lax.ppermute(upper[-1] if upper else array, axis, back))]
    gather x0 -> x4, local copies, waits for them, and re-layouts: none -> 14.4 us  [ring_gather(): blocks = blocks[(jnp.arange(size) - shift) % size]]
    transpose x0 -> x4, local copies, waits for them, and re-layouts: none -> 11.7 us  [joined_along(): return jnp.moveaxis(blocks, 0, dim).reshape(shape)]
    mul x4 -> x7, other arithmetic: 4.41 us -> 14.2 us  [local(): whole_solution = ring_gather(partial_sum, 'panel', 1) * node_mask[None, :]]
  transfers between devices with their start and end apart: 42 -> 50, of which waited for: 42 -> 50; matrix products, arithmetic and copies ran while one was open for 1% -> 1% of each run, Pallas kernels for 0% -> 0%
where the time goes in v1:
time: 941 us; the launch traced here: 931 us
  waiting for transfers between devices  586 us (62%)
  blocking collectives  139 us (15%)
  matrix products  55 us (6%)
  local copies, waits for them, and re-layouts  53.2 us (6%)
  starting transfers between devices  42.9 us (5%)
  other arithmetic  38.3 us (4%)
  between operations  17.6 us (2%)
    all_gather x4, waiting for transfers between devices, local(): lax.all_gather(target, 'panel', axis=1, tiled=True) * node_mask[None, :]  177 us
    all_to_all x8, blocking collectives, to_columns(): lax.all_to_all(full_rows, 'panel', split_axis=1, concat_axis=0, tiled=True)  139 us
    ppermute x27, waiting for transfers between devices, swapped(): return lax.ppermute(block, axis, route)  115 us
    reduce_scatter x4, waiting for transfers between devices, local(): lax.psum_scatter(contract_last(spread, inverse), 'panel', scatter_dimensi...  109 us
    ppermute x8, waiting for transfers between devices, ring_gather(): lower.append(lax.ppermute(lower[-1] if lower else array, axis, pairs))  103 us
    reduce_scatter x3, waiting for transfers between devices, local(): lax.psum_scatter(contract_last(columns, block_rows), 'panel', scatter_dim...  60.7 us
    ppermute x4, waiting for transfers between devices, ring_gather(): upper.append(lax.ppermute(upper[-1] if upper else array, axis, back))  21.4 us
    ppermute x27, starting transfers between devices, swapped(): return lax.ppermute(block, axis, route)  21.1 us
  transfers between devices with their start and end apart: 50, of which 50 were waited for; matrix products, arithmetic and copies ran while one was open for 1% of the time, Pallas kernels for 0%

profile of v1, /device:TPU:0, one launch (start us, length us, event | category | flops | bytes accessed | tf_op | source)
XLA Modules:
  0.0 931.4 jit_solution(82532490219599665)
XLA Ops:
  10.5 20.6 %all_to_all.134 = f32[64,4,512]{2,0,1:T(8,128)S(1)} all-to-all(f32[64,4,512]{2,0,1:T(8,128)S(1)} %bitcast.235), channel_id=1, replica_groups=mesh['leaf'=8,'panel'=4] {'panel'}, dimensions={1} | all-to-all | bytes 1048576 | tf_op jit(solution)/shard_map/all_to_all | solution.py:75
  31.2 7.2 fusion.79
  38.4 42.8 %reduce-scatter.8.cloned.1.call-done = f32[64,2048]{1,0:T(8,128)} async-done(((f32[256,2048]{1,0:T(8,128)}), f32[64,2048]{1,0:T(8,128)}) %reduce-scatter.8.cloned.1.call-update) | async-done | bytes 524304 | tf_op jit(solution)/shard_map/reduce_scatter | solution.py:137
  82.5 17.5 %all_to_all.135 = f32[64,4,512]{2,0,1:T(8,128)S(1)} all-to-all(f32[64,4,512]{2,0,1:T(8,128)S(1)} %bitcast.237), channel_id=1, replica_groups=mesh['leaf'=8,'panel'=4] {'panel'}, dimensions={1} | all-to-all | bytes 1048576 | tf_op jit(solution)/shard_map/all_to_all | solution.py:75
  103.2 25.9 %reduce-scatter.10.cloned.1.call-done = f32[64,1024]{1,0:T(8,128)} async-done(((f32[256,1024]{1,0:T(8,128)}), f32[64,1024]{1,0:T(8,128)}) %reduce-scatter.10.cloned.1.call-update) | async-done | bytes 262160 | tf_op jit(solution)/shard_map/reduce_scatter | solution.py:144
  136.1 17.5 %all_to_all.136 = f32[64,4,512]{2,0,1:T(8,128)S(1)} all-to-all(f32[64,4,512]{2,0,1:T(8,128)S(1)} %maximum_select_fusion), channel_id=1, replica_groups=mesh['leaf'=8,'panel'=4] {'panel'}, dimensions={1} | all-to-all | bytes 1048576 | tf_op jit(solution)/shard_map/all_to_all | solution.py:75
  156.6 26.4 %reduce-scatter.12.cloned.1.call-done = f32[64,1024]{1,0:T(8,128)} async-done(((f32[256,1024]{1,0:T(8,128)}), f32[64,1024]{1,0:T(8,128)}) %reduce-scatter.12.cloned.1.call-update) | async-done | bytes 262160 | tf_op jit(solution)/shard_map/reduce_scatter | solution.py:137
  185.8 17.5 %all_to_all.137 = f32[64,4,512]{2,0,1:T(8,128)S(1)} all-to-all(f32[64,4,512]{2,0,1:T(8,128)S(1)} %maximum_select_fusion.1), channel_id=1, replica_groups=mesh['leaf'=8,'panel'=4] {'panel'}, dimensions={1} | all-to-all | bytes 1048576 | tf_op jit(solution)/shard_map/all_to_all | solution.py:75
  207.2 19.8 %reduce-scatter.14.cloned.1.call-done = f32[64,512]{1,0:T(8,128)} async-done(((f32[256,512]{1,0:T(8,128)}), f32[64,512]{1,0:T(8,128)}) %reduce-scatter.14.cloned.1.call-update) | async-done | bytes 131088 | tf_op jit(solution)/shard_map/reduce_scatter | solution.py:144
  230.1 5.1 collective-permute-done.3
  240.7 6.9 collective-permute-done.6
  247.7 16.7 %all_to_all.138 = f32[64,4,512]{2,0,1:T(8,128)S(1)} all-to-all(f32[64,4,512]{2,0,1:T(8,128)S(1)} %maximum_select_fusion.2), channel_id=1, replica_groups=mesh['leaf'=8,'panel'=4] {'panel'}, dimensions={1} | all-to-all | bytes 1048576 | tf_op jit(solution)/shard_map/all_to_all | solution.py:75
  266.3 21.0 %reduce-scatter.16.cloned.1.call-done = f32[64,512]{1,0:T(8,128)} async-done(((f32[256,512]{1,0:T(8,128)}), f32[64,512]{1,0:T(8,128)}) %reduce-scatter.16.cloned.1.call-update) | async-done | bytes 131088 | tf_op jit(solution)/shard_map/reduce_scatter | solution.py:137
  292.0 6.1 collective-permute-done.8
  298.1 16.6 %all_to_all.139 = f32[64,4,512]{2,0,1:T(8,128)S(1)} all-to-all(f32[64,4,512]{2,0,1:T(8,128)S(1)} %maximum_select_fusion.3), channel_id=1, replica_groups=mesh['leaf'=8,'panel'=4] {'panel'}, dimensions={1} | all-to-all | bytes 1048576 | tf_op jit(solution)/shard_map/all_to_all | solution.py:75
  321.2 15.1 %reduce-scatter.18.cloned.1.call-done = f32[64,256]{1,0:T(8,128)} async-done(((f32[256,256]{1,0:T(8,128)}), f32[64,256]{1,0:T(8,128)}) %reduce-scatter.18.cloned.1.call-update) | async-done | bytes 65552 | tf_op jit(solution)/shard_map/reduce_scatter | solution.py:144
  341.6 4.9 collective-permute-done.9
  357.6 4.1 collective-permute-done.13
  363.2 6.0 collective-permute-done.14
  369.3 15.8 %all_to_all.140 = f32[64,4,512]{2,0,1:T(8,128)S(1)} all-to-all(f32[64,4,512]{2,0,1:T(8,128)S(1)} %maximum_select_fusion.4), channel_id=1, replica_groups=mesh['leaf'=8,'panel'=4] {'panel'}, dimensions={1} | all-to-all | bytes 1048576 | tf_op jit(solution)/shard_map/all_to_all | solution.py:75
  386.5 19.1 %reduce-scatter.20.cloned.1.call-done = f32[64,256]{1,0:T(8,128)} async-done(((f32[256,256]{1,0:T(8,128)}), f32[64,256]{1,0:T(8,128)}) %reduce-scatter.20.cloned.1.call-update) | async-done | bytes 65552 | tf_op jit(solution)/shard_map/reduce_scatter | solution.py:137
  409.3 4.0 collective-permute-done.16
  415.8 5.1 collective-permute-done.17
  421.0 16.5 %all_to_all.141 = f32[64,4,512]{2,0,1:T(8,128)} all-to-all(f32[64,4,512]{2,0,1:T(8,128)S(1)} %maximum_select_fusion.5), channel_id=1, replica_groups=mesh['leaf'=8,'panel'=4] {'panel'}, dimensions={1} | all-to-all | bytes 1048576 | tf_op jit(solution)/shard_map/all_to_all | solution.py:75
  439.6 44.8 %all-gather.5.cloned.1.call-done = f32[256,2048]{0,1:T(8,128)} async-done(((f32[256,512]{0,1:T(8,128)}), f32[256,2048]{0,1:T(8,128)}) %all-gather.5.cloned.1.call-update) | async-done | bytes 2097168 | tf_op jit(solution)/shard_map/all_gather | solution.py:180
  489.8 12.5 %collective-permute-done.19 = f32[256,512]{1,0:T(8,128)S(1)} collective-permute-done((f32[256,512]{1,0:T(8,128)S(1)}, f32[256,512]{1,0:T(8,128)S(1)}, u32[]{:S(2)}, u32[]{:S(2)}) %collective-permute-start.19) | collective-permute-done | bytes 524320 | tf_op jit(solution)/shard_map/ppermute | solution.py:40
  504.0 11.6 %collective-permute-done.20 = f32[256,512]{1,0:T(8,128)S(1)} collective-permute-done((f32[256,512]{1,0:T(8,128)S(1)}, f32[256,512]{1,0:T(8,128)S(1)}, u32[]{:S(2)}, u32[]{:S(2)}) %collective-permute-start.20) | collective-permute-done | bytes 524320 | tf_op jit(solution)/shard_map/ppermute | solution.py:40
  516.6 3.7 collective-permute-start.23
  520.3 13.1 %collective-permute-done.21 = f32[256,512]{1,0:T(8,128)} collective-permute-done((f32[256,512]{1,0:T(8,128)}, f32[256,512]{1,0:T(8,128)}, u32[]{:S(2)}, u32[]{:S(2)}) %collective-permute-start.21) | collective-permute-done | bytes 524320 | tf_op jit(solution)/shard_map/ppermute | solution.py:24
  533.4 5.3 collective-permute-start.22
  540.9 12.4 %collective-permute-done.22 = f32[256,512]{1,0:T(8,128)} collective-permute-done((f32[256,512]{1,0:T(8,128)}, f32[256,512]{1,0:T(8,128)}, u32[]{:S(2)}, u32[]{:S(2)}) %collective-permute-start.22) | collective-permute-done | bytes 524320 | tf_op jit(solution)/shard_map/ppermute | solution.py:24
  575.9 12.5 %collective-permute-done.25 = f32[256,512]{1,0:T(8,128)S(1)} collective-permute-done((f32[256,512]{1,0:T(8,128)S(1)}, f32[256,512]{1,0:T(8,128)S(1)}, u32[]{:S(2)}, u32[]{:S(2)}) %collective-permute-start.25) | collective-permute-done | bytes 524320 | tf_op jit(solution)/shard_map/ppermute | solution.py:40
  589.4 43.9 %all-gather.7.cloned.1.call-done = f32[256,2048]{1,0:T(8,128)} async-done(((f32[256,512]{1,0:T(8,128)}), f32[256,2048]{1,0:T(8,128)}) %all-gather.7.cloned.1.call-update) | async-done | bytes 2097168 | tf_op jit(solution)/shard_map/all_gather | solution.py:180
  639.4 12.5 %collective-permute-done.27 = f32[256,512]{1,0:T(8,128)S(1)} collective-permute-done((f32[256,512]{1,0:T(8,128)S(1)}, f32[256,512]{1,0:T(8,128)S(1)}, u32[]{:S(2)}, u32[]{:S(2)}) %collective-permute-start.27) | collective-permute-done | bytes 524320 | tf_op jit(solution)/shard_map/ppermute | solution.py:40
  652.2 3.7 collective-permute-start.30
  655.9 12.8 %collective-permute-done.28 = f32[256,512]{1,0:T(8,128)S(1)} collective-permute-done((f32[256,512]{1,0:T(8,128)S(1)}, f32[256,512]{1,0:T(8,128)S(1)}, u32[]{:S(2)}, u32[]{:S(2)}) %collective-permute-start.28) | collective-permute-done | bytes 524320 | tf_op jit(solution)/shard_map/ppermute | solution.py:24
  668.7 7.8 collective-permute-done.30
  676.5 13.0 %collective-permute-done.29 = f32[256,512]{1,0:T(8,128)S(1)} collective-permute-done((f32[256,512]{1,0:T(8,128)S(1)}, f32[256,512]{1,0:T(8,128)S(1)}, u32[]{:S(2)}, u32[]{:S(2)}) %collective-permute-start.29) | collective-permute-done | bytes 524320 | tf_op jit(solution)/shard_map/ppermute | solution.py:24
  711.8 43.9 %all-gather.9.cloned.1.call-done = f32[256,2048]{1,0:T(8,128)} async-done(((f32[256,512]{1,0:T(8,128)}), f32[256,2048]{1,0:T(8,128)}) %all-gather.9.cloned.1.call-update) | async-done | bytes 2097168 | tf_op jit(solution)/shard_map/all_gather | solution.py:180
  761.2 3.7 collective-permute-start.35
  764.9 12.8 %collective-permute-done.33 = f32[256,512]{1,0:T(8,128)S(1)} collective-permute-done((f32[256,512]{1,0:T(8,128)S(1)}, f32[256,512]{1,0:T(8,128)S(1)}, u32[]{:S(2)}, u32[]{:S(2)}) %collective-permute-start.33) | collective-permute-done | bytes 524320 | tf_op jit(solution)/shard_map/ppermute | solution.py:24
  777.9 8.4 collective-permute-done.35
  786.3 13.0 %collective-permute-done.34 = f32[256,512]{1,0:T(8,128)S(1)} collective-permute-done((f32[256,512]{1,0:T(8,128)S(1)}, f32[256,512]{1,0:T(8,128)S(1)}, u32[]{:S(2)}, u32[]{:S(2)}) %collective-permute-start.34) | collective-permute-done | bytes 524320 | tf_op jit(solution)/shard_map/ppermute | solution.py:24
  822.4 44.0 %all-gather.11.cloned.1.call-done = f32[256,2048]{1,0:T(8,128)} async-done(((f32[256,512]{1,0:T(8,128)}), f32[256,2048]{1,0:T(8,128)}) %all-gather.11.cloned.1.call-update) | async-done | bytes 2097168 | tf_op jit(solution)/shard_map/all_gather | solution.py:180
  866.3 6.4 fusion
  873.0 3.7 collective-permute-start.38
  876.7 12.8 %collective-permute-done.36 = f32[256,512]{1,0:T(8,128)S(1)} collective-permute-done((f32[256,512]{1,0:T(8,128)S(1)}, f32[256,512]{1,0:T(8,128)S(1)}, u32[]{:S(2)}, u32[]{:S(2)}) %collective-permute-start.36) | collective-permute-done | bytes 524320 | tf_op jit(solution)/shard_map/ppermute | solution.py:24
  897.7 13.0 %collective-permute-done.37 = f32[256,512]{1,0:T(8,128)} collective-permute-done((f32[256,512]{1,0:T(8,128)S(1)}, f32[256,512]{1,0:T(8,128)}, u32[]{:S(2)}, u32[]{:S(2)}) %collective-permute-start.37) | collective-permute-done | bytes 524320 | tf_op jit(solution)/shard_map/ppermute | solution.py:24
  (253 shorter events, 184.5 us)
Async XLA Ops:
  7.2 74.1 %reduce-scatter.8.cloned.1.call-start = ((), (), s32[]{:S(2)}) async-start(), calls=%async_computation.15 | async-start | bytes 2621440 | tf_op jit(solution)/shard_map/reduce_scatter | solution.py:137
  38.3 90.8 %reduce-scatter.10.cloned.1.call-start = ((), (), s32[]{:S(2)}) async-start(), calls=%async_computation.16 | async-start | bytes 1310720 | tf_op jit(solution)/shard_map/reduce_scatter | solution.py:144
  103.0 80.1 %reduce-scatter.12.cloned.1.call-start = ((), (), s32[]{:S(2)}) async-start(), calls=%async_computation.17 | async-start | bytes 1310720 | tf_op jit(solution)/shard_map/reduce_scatter | solution.py:137
  131.5 1.9 collective-permute-start
  134.5 1.6 collective-permute-start.1
  156.6 70.4 %reduce-scatter.14.cloned.1.call-start = ((), (), s32[]{:S(2)}) async-start(), calls=%async_computation.18 | async-start | bytes 655360 | tf_op jit(solution)/shard_map/reduce_scatter | solution.py:144
  184.1 1.6 collective-permute-start.2
  205.9 81.3 %reduce-scatter.16.cloned.1.call-start = ((), (), s32[]{:S(2)}) async-start(), calls=%async_computation.19 | async-start | bytes 655360 | tf_op jit(solution)/shard_map/reduce_scatter | solution.py:137
  228.7 6.5 collective-permute-start.3
  235.3 1.4 collective-permute-start.4
  237.7 1.4 collective-permute-start.5
  239.1 8.5 collective-permute-start.6
  266.2 70.0 %reduce-scatter.18.cloned.1.call-start = ((), (), s32[]{:S(2)}) async-start(), calls=%async_computation.20 | async-start | bytes 327680 | tf_op jit(solution)/shard_map/reduce_scatter | solution.py:144
  288.2 1.4 collective-permute-start.7
  289.6 8.4 collective-permute-start.8
  317.1 88.5 %reduce-scatter.20.cloned.1.call-start = ((), (), s32[]{:S(2)}) async-start(), calls=%async_computation.21 | async-start | bytes 327680 | tf_op jit(solution)/shard_map/reduce_scatter | solution.py:137
  340.1 6.4 collective-permute-start.9
  347.2 5.2 collective-permute-start.10
  352.5 1.3 collective-permute-start.11
  356.0 5.6 collective-permute-start.13
  361.6 7.6 collective-permute-start.14
  386.4 98.0 %all-gather.5.cloned.1.call-start = ((), (), s32[]{:S(2)}) async-start(), calls=%async_computation.22 | async-start | bytes 2621440 | tf_op jit(solution)/shard_map/all_gather | solution.py:180
  407.7 5.6 collective-permute-start.16
  413.4 7.6 collective-permute-start.17
  439.6 193.8 %all-gather.7.cloned.1.call-start = ((), (), s32[]{:S(2)}) async-start(), calls=%async_computation.23 | async-start | bytes 2621440 | tf_op jit(solution)/shard_map/all_gather | solution.py:180
  486.3 2.0 collective-permute-start.18
  488.3 14.0 %collective-permute-start.19 = (f32[256,512]{1,0:T(8,128)S(1)}, f32[256,512]{1,0:T(8,128)S(1)}, u32[]{:S(2)}, u32[]{:S(2)}) collective-permute-start(f32[256,512]{1,0:T(8,128)S(1)} %add.326), channel_id=1, source_target_pairs={{0,8},{8,0},{4,12},{12,4},{16,24},{24,16},{20,28},{28,20},{1,9},{9... | collective-permute-start | bytes 1572872 | tf_op jit(solution)/shard_map/ppermute | solution.py:40
  502.4 13.2 %collective-permute-start.20 = (f32[256,512]{1,0:T(8,128)S(1)}, f32[256,512]{1,0:T(8,128)S(1)}, u32[]{:S(2)}, u32[]{:S(2)}) collective-permute-start(f32[256,512]{1,0:T(8,128)S(1)} %add.327), channel_id=1, source_target_pairs={{0,16},{16,0},{4,20},{20,4},{8,24},{24,8},{12,28},{28,12},{1,17},{... | collective-permute-start | bytes 1572872 | tf_op jit(solution)/shard_map/ppermute | solution.py:40
  516.5 16.9 %collective-permute-start.21 = (f32[256,512]{1,0:T(8,128)}, f32[256,512]{1,0:T(8,128)}, u32[]{:S(2)}, u32[]{:S(2)}) collective-permute-start(f32[256,512]{1,0:T(8,128)} %add.328), channel_id=1, source_target_pairs={{0,1},{1,2},{2,3},{3,0},{4,5},{5,6},{6,7},{7,4},{8,9},{9,10},{10,1... | collective-permute-start | bytes 1572872 | tf_op jit(solution)/shard_map/ppermute | solution.py:24
  516.6 24.3 %collective-permute-start.23 = (f32[256,512]{1,0:T(8,128)}, f32[256,512]{1,0:T(8,128)}, u32[]{:S(2)}, u32[]{:S(2)}) collective-permute-start(f32[256,512]{1,0:T(8,128)} %add.328), channel_id=1, source_target_pairs={{1,0},{2,1},{3,2},{0,3},{5,4},{6,5},{7,6},{4,7},{9,8},{10,9},{11,1... | collective-permute-start | bytes 1572872 | tf_op jit(solution)/shard_map/ppermute | solution.py:26
  533.4 20.0 %collective-permute-start.22 = (f32[256,512]{1,0:T(8,128)}, f32[256,512]{1,0:T(8,128)}, u32[]{:S(2)}, u32[]{:S(2)}) collective-permute-start(f32[256,512]{1,0:T(8,128)} %collective-permute-done.21), channel_id=1, source_target_pairs={{0,1},{1,2},{2,3},{3,0},{4,5},{5,6},{6,7},{7,4},{8,9},{9,10},{10,1... | collective-permute-start | bytes 1572872 | tf_op jit(solution)/shard_map/ppermute | solution.py:24
  572.3 2.0 collective-permute-start.24
  574.4 14.0 %collective-permute-start.25 = (f32[256,512]{1,0:T(8,128)S(1)}, f32[256,512]{1,0:T(8,128)S(1)}, u32[]{:S(2)}, u32[]{:S(2)}) collective-permute-start(f32[256,512]{1,0:T(8,128)S(1)} %add.331), channel_id=1, source_target_pairs={{0,8},{8,0},{4,12},{12,4},{16,24},{24,16},{20,28},{28,20},{1,9},{9... | collective-permute-start | bytes 1572872 | tf_op jit(solution)/shard_map/ppermute | solution.py:40
  589.4 166.4 %all-gather.9.cloned.1.call-start = ((), (), s32[]{:S(2)}) async-start(), calls=%async_computation.24 | async-start | bytes 2621440 | tf_op jit(solution)/shard_map/all_gather | solution.py:180
  635.8 2.0 collective-permute-start.26
  637.9 14.0 %collective-permute-start.27 = (f32[256,512]{1,0:T(8,128)S(1)}, f32[256,512]{1,0:T(8,128)S(1)}, u32[]{:S(2)}, u32[]{:S(2)}) collective-permute-start(f32[256,512]{1,0:T(8,128)S(1)} %add.333), channel_id=1, source_target_pairs={{0,8},{8,0},{4,12},{12,4},{16,24},{24,16},{20,28},{28,20},{1,9},{9... | collective-permute-start | bytes 1572872 | tf_op jit(solution)/shard_map/ppermute | solution.py:40
  652.0 16.6 %collective-permute-start.28 = (f32[256,512]{1,0:T(8,128)S(1)}, f32[256,512]{1,0:T(8,128)S(1)}, u32[]{:S(2)}, u32[]{:S(2)}) collective-permute-start(f32[256,512]{1,0:T(8,128)S(1)} %add.334), channel_id=1, source_target_pairs={{0,1},{1,2},{2,3},{3,0},{4,5},{5,6},{6,7},{7,4},{8,9},{9,10},{10,1... | collective-permute-start | bytes 1572872 | tf_op jit(solution)/shard_map/ppermute | solution.py:24
  652.2 24.2 %collective-permute-start.30 = (f32[256,512]{1,0:T(8,128)S(1)}, f32[256,512]{1,0:T(8,128)S(1)}, u32[]{:S(2)}, u32[]{:S(2)}) collective-permute-start(f32[256,512]{1,0:T(8,128)S(1)} %add.334), channel_id=1, source_target_pairs={{1,0},{2,1},{3,2},{0,3},{5,4},{6,5},{7,6},{4,7},{9,8},{10,9},{11,1... | collective-permute-start | bytes 1572872 | tf_op jit(solution)/shard_map/ppermute | solution.py:26
  668.6 20.8 %collective-permute-start.29 = (f32[256,512]{1,0:T(8,128)S(1)}, f32[256,512]{1,0:T(8,128)S(1)}, u32[]{:S(2)}, u32[]{:S(2)}) collective-permute-start(f32[256,512]{1,0:T(8,128)S(1)} %collective-permute-done.28), channel_id=1, source_target_pairs={{0,1},{1,2},{2,3},{3,0},{4,5},{5,6},{6,7},{7,4},{8,9},{9,10},{10,1... | collective-permute-start | bytes 1572872 | tf_op jit(solution)/shard_map/ppermute | solution.py:24
  708.9 2.0 collective-permute-start.31
  711.8 154.5 %all-gather.11.cloned.1.call-start = ((), (), s32[]{:S(2)}) async-start(), calls=%async_computation.25 | async-start | bytes 2621440 | tf_op jit(solution)/shard_map/all_gather | solution.py:180
  758.9 2.0 collective-permute-start.32
  761.0 16.7 %collective-permute-start.33 = (f32[256,512]{1,0:T(8,128)S(1)}, f32[256,512]{1,0:T(8,128)S(1)}, u32[]{:S(2)}, u32[]{:S(2)}) collective-permute-start(f32[256,512]{1,0:T(8,128)S(1)} %add.338), channel_id=1, source_target_pairs={{0,1},{1,2},{2,3},{3,0},{4,5},{5,6},{6,7},{7,4},{8,9},{9,10},{10,1... | collective-permute-start | bytes 1572872 | tf_op jit(solution)/shard_map/ppermute | solution.py:24
  761.2 25.1 %collective-permute-start.35 = (f32[256,512]{1,0:T(8,128)S(1)}, f32[256,512]{1,0:T(8,128)S(1)}, u32[]{:S(2)}, u32[]{:S(2)}) collective-permute-start(f32[256,512]{1,0:T(8,128)S(1)} %add.338), channel_id=1, source_target_pairs={{1,0},{2,1},{3,2},{0,3},{5,4},{6,5},{7,6},{4,7},{9,8},{10,9},{11,1... | collective-permute-start | bytes 1572872 | tf_op jit(solution)/shard_map/ppermute | solution.py:26
  777.7 21.6 %collective-permute-start.34 = (f32[256,512]{1,0:T(8,128)S(1)}, f32[256,512]{1,0:T(8,128)S(1)}, u32[]{:S(2)}, u32[]{:S(2)}) collective-permute-start(f32[256,512]{1,0:T(8,128)S(1)} %collective-permute-done.33), channel_id=1, source_target_pairs={{0,1},{1,2},{2,3},{3,0},{4,5},{5,6},{6,7},{7,4},{8,9},{9,10},{10,1... | collective-permute-start | bytes 1572872 | tf_op jit(solution)/shard_map/ppermute | solution.py:24
  872.8 16.7 %collective-permute-start.36 = (f32[256,512]{1,0:T(8,128)S(1)}, f32[256,512]{1,0:T(8,128)S(1)}, u32[]{:S(2)}, u32[]{:S(2)}) collective-permute-start(f32[256,512]{1,0:T(8,128)S(1)} %fusion), channel_id=1, source_target_pairs={{0,1},{1,2},{2,3},{3,0},{4,5},{5,6},{6,7},{7,4},{8,9},{9,10},{10,1... | collective-permute-start | bytes 1572872 | tf_op jit(solution)/shard_map/ppermute | solution.py:24
  873.0 24.7 %collective-permute-start.38 = (f32[256,512]{1,0:T(8,128)S(1)}, f32[256,512]{1,0:T(8,128)}, u32[]{:S(2)}, u32[]{:S(2)}) collective-permute-start(f32[256,512]{1,0:T(8,128)S(1)} %fusion), channel_id=1, source_target_pairs={{1,0},{2,1},{3,2},{0,3},{5,4},{6,5},{7,6},{4,7},{9,8},{10,9},{11,1... | collective-permute-start | bytes 1572872 | tf_op jit(solution)/shard_map/ppermute | solution.py:26
  889.4 21.3 %collective-permute-start.37 = (f32[256,512]{1,0:T(8,128)S(1)}, f32[256,512]{1,0:T(8,128)}, u32[]{:S(2)}, u32[]{:S(2)}) collective-permute-start(f32[256,512]{1,0:T(8,128)S(1)} %collective-permute-done.36), channel_id=1, source_target_pairs={{0,1},{1,2},{2,3},{3,0},{4,5},{5,6},{6,7},{7,4},{8,9},{9,10},{10,1... | collective-permute-start | bytes 1572872 | tf_op jit(solution)/shard_map/ppermute | solution.py:24
  (26 other events, 416.8 us)
Sparse Core Ops, SparseCore 0:
  38.5 42.7 reduce-scatter.7
  103.1 25.9 reduce-scatter.9
  156.7 26.3 reduce-scatter.11
  206.1 20.9 reduce-scatter.13
  266.4 20.8 reduce-scatter.15
  317.3 18.9 reduce-scatter.17
  386.6 19.0 reduce-scatter.19
  439.7 44.7 all-gather.4
  589.5 43.7 all-gather.6
  711.9 43.7 all-gather.8
  822.5 43.7 all-gather.10
